TPU v7x, 32 devices: a whole 2x2x4 slice. The times are simulated.
32 devices in a mesh: zone: 4 (over y, x), dev: 8 (over z, core).
Axes of the slice: x: 2, y: 2, z: 4, core: 2. Of those that a mesh axis runs over, the one named last changes fastest.
Arguments:
- quad_weight: float32 [16384, 128], P(('zone', 'dev')), may hold values from 0.002 to 0.014
- param_coords: float32 [16384, 4, 128], P(('zone', 'dev')), may hold values from -1 to 1
- slave_points: float32 [16384, 3, 128], P(('zone', 'dev')), may hold values from -6 to 6
- slave_normals: float32 [16384, 3, 128], P(('zone', 'dev')), may hold values from -1 to 1, as said below
- block_owner: int32 [16384, 1], P(('zone', 'dev')), may hold values from 0 to 7; in each aligned block of 128 rows (0 to 127, 128 to 255, ...) at most 16 rows name the same one
- block_patch: int32 [16384], P(('zone', 'dev')), may hold values from 0 to 8191
- block_count: int32 [32, 4], P(('zone', 'dev')), may hold values from 1 to 128, as said below
- active_flags: int32 [4, 16384], P(None, ('zone', 'dev')), may hold values 0 or 1
- normal_mult: float32 [4, 16384], P(None, ('zone', 'dev')), may hold values from 0.5 to 4
- tangent_mult: float32 [12, 16384], P(None, ('zone', 'dev')), may hold values from -6 to 6
- master_patch: float32 [12, 262144], P(None, ('zone', 'dev')), may hold values from -6 to 6
Outputs:
- mortar_d: float32 [16, 16384], P(None, ('zone', 'dev'))
- mortar_m: float32 [16, 16384], P(None, ('zone', 'dev'))
- gap_lin: float32 [48, 16384], P(None, ('zone', 'dev'))
- gap_res: float32 [4, 16384], P(None, ('zone', 'dev'))
- cone_res: float32 [12, 16384], P(None, ('zone', 'dev'))
Inputs may be any that keep to these rules, and one draw needn't show every extreme that they name: Device q's live blocks toward group k are the first block_count[q, k] of its 128 slots for k; in every draw each device fills all 128 slots toward one group, the same group for all devices of one dev index. `slave_normals`: every normal has unit length. `block_owner`: in each aligned block of 128 slots (one device toward one group) no owner is named by more than 16 slots.
All inputs are finite; a program needn't handle non-finite values. No bound on the sum of `active_flags` on one device may be relied on, other than what follows from the above.
Results may differ from a plain program's by a relative error of at most 0.0003.
Values sent between devices are 32-bit elements; how exact they have to be, the bound alone decides.
A program may use at most 320 MiB of HBM per device.

v0:
```python
import jax
import jax.numpy as jnp
from jax import lax
from jax.sharding import PartitionSpec as P

BUCKET = 16


friction_coef = 0.3
newton_scale = 4.0


def bilinear(first, second):
    return jnp.stack(
        [
            0.25 * (1.0 - first) * (1.0 - second),
            0.25 * (1.0 + first) * (1.0 - second),
            0.25 * (1.0 + first) * (1.0 + second),
            0.25 * (1.0 - first) * (1.0 + second),
        ],
        axis=0,
    )


def slave_terms(weight, coords):
    shape_s = bilinear(coords[:, 2], coords[:, 3])
    weighted = weight[None] * shape_s
    return jnp.sum(weighted[:, None] * shape_s[None], axis=-1).reshape(16, -1)


def master_terms(weight, coords, points, normals, corners):
    shape_s = bilinear(coords[:, 2], coords[:, 3])
    shape_m = bilinear(coords[:, 0], coords[:, 1])
    weighted = weight[None] * shape_s
    paired = weighted[:, None] * shape_m[None]
    mortar_m = jnp.sum(paired, axis=-1).reshape(16, -1)
    diffs = []
    for direction in range(3):
        position = jnp.sum(shape_m * corners[4 * direction : 4 * direction + 4][:, :, None], axis=0)
        diffs.append(position - points[:, direction])
    gap_point = normals[:, 0] * diffs[0] + normals[:, 1] * diffs[1] + normals[:, 2] * diffs[2]
    wgap = jnp.sum(weighted * gap_point[None], axis=-1)
    slips = [
        jnp.sum(weighted * (diffs[direction] - normals[:, direction] * gap_point)[None], axis=-1)
        for direction in range(3)
    ]
    lins = [
        jnp.sum(paired * normals[:, direction][None, None], axis=-1).reshape(16, -1)
        for direction in range(3)
    ]
    return (mortar_m, wgap, jnp.concatenate(slips, axis=0), jnp.concatenate(lins, axis=0))


def residuals(wgap, wslip, active, normal_mult, tangent_mult):
    radius = friction_coef * normal_mult
    trial = tangent_mult + newton_scale * wslip
    length = jnp.sqrt(trial[0:4] * trial[0:4] + trial[4:8] * trial[4:8] + trial[8:12] * trial[8:12])
    factor = radius / jnp.maximum(radius, length)
    factor_all = jnp.concatenate([factor, factor, factor], axis=0)
    active_all = jnp.concatenate([active, active, active], axis=0)
    cone = jnp.where(active_all == 1, tangent_mult - factor_all * trial, tangent_mult)
    gap = jnp.where(active == 1, wgap, normal_mult)
    return (gap, cone)


def live_slots(counts, slots, groups):
    cap = slots // groups
    index = jnp.arange(slots, dtype=jnp.int32)
    group_of = index // cap
    per_slot = jnp.sum(
        jnp.where(
            group_of[:, None] == jnp.arange(groups, dtype=jnp.int32)[None, :], counts[None, :], 0
        ),
        axis=1,
    )
    return index % cap < per_slot


def lookup(owner, offset, master_patch):
    count = owner.shape[0]
    peers = lax.axis_size("dev")
    sources = lax.axis_size("zone")
    width = sources * BUCKET
    block = count // sources
    peer_index = jnp.arange(peers, dtype=jnp.int32)
    hits = (owner.reshape(sources, block)[:, :, None] == peer_index[None, None, :]).astype(
        jnp.int32
    )
    before = jnp.cumsum(hits, axis=1) - hits
    rank = jnp.sum(before * hits, axis=2)
    position = (jnp.arange(sources, dtype=jnp.int32)[:, None] * BUCKET + rank).reshape(count)
    table = jnp.zeros((peers, width), jnp.int32).at[owner, position].set(offset)
    found = jnp.take(
        master_patch, lax.all_to_all(table, "dev", split_axis=0, concat_axis=0, tiled=True), axis=1
    )
    replies = lax.all_to_all(found, "dev", split_axis=1, concat_axis=1, tiled=True)
    flat = replies.reshape(12, peers * width)
    return jnp.take(flat, owner * width + position, axis=1)


def local(
    quad_weight,
    param_coords,
    slave_points,
    slave_normals,
    block_owner,
    block_patch,
    block_count,
    active_flags,
    normal_mult,
    tangent_mult,
    master_patch,
):
    groups = lax.axis_size("zone")
    slots = quad_weight.shape[0]
    mortar_d = slave_terms(quad_weight, param_coords)
    owner_ids = block_owner[:, 0]
    asked_owner, asked_patch = (
        lax.all_to_all(owner_ids, "zone", split_axis=0, concat_axis=0, tiled=True),
        lax.all_to_all(block_patch, "zone", split_axis=0, concat_axis=0, tiled=True),
    )
    found = lookup(asked_owner, asked_patch, master_patch)
    corners = lax.all_to_all(found, "zone", split_axis=1, concat_axis=1, tiled=True)
    back_m, back_gap, back_slip, back_lin = master_terms(
        quad_weight, param_coords, slave_points, slave_normals, corners
    )
    gap, cone = residuals(back_gap, back_slip, active_flags, normal_mult, tangent_mult)
    live = live_slots(block_count[0], slots, groups)[None]
    return (
        jnp.where(live, mortar_d, 0.0),
        jnp.where(live, back_m, 0.0),
        jnp.where(live, back_lin, 0.0),
        jnp.where(live, gap, 0.0),
        jnp.where(live, cone, 0.0),
    )


def solution(mesh):
    placed = (
        P(("zone", "dev"), None),
        P(("zone", "dev"), None, None),
        P(("zone", "dev"), None, None),
        P(("zone", "dev"), None, None),
        P(("zone", "dev"), None),
        P(("zone", "dev")),
        P(("zone", "dev"), None),
        P(None, ("zone", "dev")),
        P(None, ("zone", "dev")),
        P(None, ("zone", "dev")),
        P(None, ("zone", "dev")),
    )
    return jax.shard_map(
        local,
        mesh=mesh,
        in_specs=placed,
        out_specs=(
            P(None, ("zone", "dev")),
            P(None, ("zone", "dev")),
            P(None, ("zone", "dev")),
            P(None, ("zone", "dev")),
            P(None, ("zone", "dev")),
        ),
        check_vma=False,
    )
```

profile of v0, /device:TPU:0, one launch (start us, length us, event | category | flops | bytes accessed | tf_op | source)
XLA Modules:
  0.0 147.0 jit_solution(7890981640103569913)
XLA Ops:
  0.6 5.2 %all-to-all-start = ((s32[4,128,1]{1,2,0:T(1,128)}), s32[4,128,1]{1,2,0:T(1,128)S(1)}, u32[]{:S(2)}, u32[]{:S(2)}) async-start(s32[4,128,1]{1,2,0:T(1,128)} %bitcast.121), calls=%async_computation | async-start | bytes 4096 | tf_op jit(solution)/shard_map/all_to_all | solution.py:119
  5.8 3.4 %fusion.17 = (f32[512,1,128]{2,1,0:T(1,128)S(1)}, f32[512,1,128]{2,1,0:T(1,128)S(1)}, f32[512,1,128]{2,1,0:T(1,128)S(1)}, f32[512,1,128]{2,1,0:T(1,128)S(1)}) fusion(f32[512,4,128]{2,1,0:T(4,128)} %param.12), kind=kLoop, calls=%fused_computation.99 | loop fusion | bytes 2097152 | tf_op jit(solution)/shard_map/slice | solution.py:26
  9.2 1.2 slice_bitcast_fusion.1
  10.4 1.1 multiply_bitcast_fusion.3
  11.5 0.8 multiply_bitcast_fusion.7
  12.3 4.2 %all-to-all-start.1 = ((s32[4,128,1]{1,2,0:T(1,128)}), s32[4,128,1]{1,2,0:T(1,128)S(1)}, u32[]{:S(2)}, u32[]{:S(2)}) async-start(s32[4,128,1]{1,2,0:T(1,128)} %bitcast.18), calls=%async_computation.1 | async-start | bytes 4096 | tf_op jit(solution)/shard_map/all_to_all | solution.py:120
  16.6 0.3 reduce_window_sum.11
  16.9 0.2 select_reduce_fusion
  17.2 3.8 %all-to-all-done.1 = s32[4,128,1]{1,2,0:T(1,128)S(1)} async-done(((s32[4,128,1]{1,2,0:T(1,128)}), s32[4,128,1]{1,2,0:T(1,128)S(1)}, u32[]{:S(2)}, u32[]{:S(2)}) %all-to-all-start.1) | async-done | bytes 2080 | tf_op jit(solution)/shard_map/all_to_all | solution.py:120
  21.0 0.6 broadcast_in_dim.120
  21.6 76.9 %scatter_fusion = s32[8,64]{1,0:T(8,128)} fusion(s32[8,64]{1,0:T(8,128)} %broadcast_in_dim.120, s32[512]{0:T(512)S(1)} %bitcast.104, s32[512]{0:T(512)S(1)} %bitcast.118), kind=kCustom, calls=%fused_computation.2 | custom fusion | bytes 10240 | tf_op jit(solution)/shard_map/scatter | solution.py:92
  98.5 4.9 %all-to-all-start.2 = ((s32[8,1,64]{2,1,0:T(1,128)}), s32[8,1,64]{2,1,0:T(1,128)S(1)}, u32[]{:S(2)}, u32[]{:S(2)}) async-start(s32[8,1,64]{2,1,0:T(1,128)} %bitcast.21), calls=%async_computation.2 | async-start | bytes 8192 | tf_op jit(solution)/shard_map/all_to_all | solution.py:94
  103.5 3.6 %copy.70 = f32[12,8192]{0,1:T(8,128)} copy(f32[12,8192]{1,0:T(8,128)} %param.21) | data formatting | bytes 786432 | tf_op args[10]
  107.1 1.8 %all-to-all-done.2 = s32[8,1,64]{2,1,0:T(1,128)S(1)} async-done(((s32[8,1,64]{2,1,0:T(1,128)}), s32[8,1,64]{2,1,0:T(1,128)S(1)}, u32[]{:S(2)}, u32[]{:S(2)}) %all-to-all-start.2) | async-done | bytes 2080 | tf_op jit(solution)/shard_map/all_to_all | solution.py:94
  108.9 3.2 %gather_fusion = f32[512,12]{1,0:T(8,128)S(1)} fusion(f32[12,8192]{0,1:T(8,128)} %copy.70, s32[1024]{0:T(1024)S(1)} %pad_clamp_fusion.1), kind=kCustom, calls=%fused_computation | custom fusion | bytes 51200 | tf_op jit(solution)/shard_map/jit(_take)/gather | solution.py:93
  112.3 0.7 reshape.593
  113.0 3.3 %all-to-all-start.3 = ((f32[8,1,768]{2,1,0:T(1,128)}), f32[8,1,768]{2,1,0:T(1,128)S(1)}, u32[]{:S(2)}, u32[]{:S(2)}) async-start(f32[8,1,768]{2,1,0:T(1,128)} %reshape.593), calls=%async_computation.3 | async-start | bytes 49152 | tf_op jit(solution)/shard_map/all_to_all | solution.py:96
  116.4 5.7 %all-to-all-done.3 = f32[8,1,768]{2,1,0:T(1,128)S(1)} async-done(((f32[8,1,768]{2,1,0:T(1,128)}), f32[8,1,768]{2,1,0:T(1,128)S(1)}, u32[]{:S(2)}, u32[]{:S(2)}) %all-to-all-start.3) | async-done | bytes 24608 | tf_op jit(solution)/shard_map/all_to_all | solution.py:96
  122.1 0.5 broadcast.412
  122.6 0.7 reduce
  123.5 1.6 %gather_fusion.1 = f32[512,12]{1,0:T(8,128)} fusion(f32[12,512]{0,1:T(8,128)S(1)} %bitcast.105, s32[1024]{0:T(1024)S(1)} %pad_clamp_fusion), kind=kCustom, calls=%fused_computation.1 | custom fusion | bytes 51200 | tf_op jit(solution)/shard_map/jit(_take)/gather | solution.py:98
  125.2 1.1 copy.73
  126.2 0.6 broadcast_select_fusion
  126.9 3.3 %all-to-all-start.4 = ((f32[12,4,128]{2,0,1:T(8,128)}), f32[12,4,128]{2,0,1:T(8,128)S(1)}, u32[]{:S(2)}, u32[]{:S(2)}) async-start(f32[12,4,128]{2,0,1:T(8,128)} %broadcast_select_fusion), calls=%async_computation.4 | async-start | bytes 65536 | tf_op jit(solution)/shard_map/all_to_all | solution.py:123
  130.2 4.7 %all-to-all-done.4 = f32[12,4,128]{2,0,1:T(8,128)S(1)} async-done(((f32[12,4,128]{2,0,1:T(8,128)}), f32[12,4,128]{2,0,1:T(8,128)S(1)}, u32[]{:S(2)}, u32[]{:S(2)}) %all-to-all-start.4) | async-done | bytes 24608 | tf_op jit(solution)/shard_map/all_to_all | solution.py:123
  134.9 2.2 %multiply_reduce_fusion.6 = (f32[512,128]{1,0:T(8,128)S(1)}, f32[512,128]{1,0:T(8,128)S(1)}, f32[512,128]{1,0:T(8,128)S(1)}, f32[4,512,128]{2,1,0:T(8,128)S(1)}) fusion(f32[4,512]{1,0:T(4,128)S(1)} %get-tuple-element.42, f32[1,512,128]{2,1,0:T(8,128)} %get-tuple-element.39, f32[1,512,128]{2,1,0:T(8,128)} %get-tuple-element.40, ...), kind=kLoop, calls=%fused_computation.17 | loop fusion | flops 2162688 | bytes 2908160 | tf_op jit(solution)/shard_map/reduce_sum | solution.py:39
  137.4 1.3 multiply_reduce_fusion.4
  138.8 0.6 maximum_divide_fusion
  139.4 0.6 fusion.4
  140.0 5.6 %fusion = (f32[4,4,512]{2,1,0:T(4,128)S(1)}, f32[4,4,512]{2,1,0:T(4,128)S(1)}, f32[4,4,512]{2,1,0:T(4,128)S(1)}, f32[4,4,512]{2,1,0:T(4,128)S(1)}, f32[4,4,512]{2,1,0:T(4,128)S(1)}) fusion(f32[512,128]{1,0:T(8,128)S(1)} %get-tuple-element.31, f32[4,512,128]{2,1,0:T(8,128)S(1)} %get-tuple-element.29, f32[4,512,128]{2,1,0:T(8,128)S(1)} %get-tuple-element.17, ...), kind=kLoop, calls=%fused_computation.7 | loop fusion | flops 10444800 | bytes 4096000 | tf_op jit(solution)/shard_map/reduce_sum | solution.py:48
  145.7 0.6 broadcast_select_fusion.1
  146.4 0.6 maximum_select_fusion
  (42 shorter events, 1.2 us)
Async XLA Ops:
  0.6 11.6 %all-to-all-start = ((s32[4,128,1]{1,2,0:T(1,128)}), s32[4,128,1]{1,2,0:T(1,128)S(1)}, u32[]{:S(2)}, u32[]{:S(2)}) async-start(s32[4,128,1]{1,2,0:T(1,128)} %bitcast.121), calls=%async_computation | async-start | bytes 4096 | tf_op jit(solution)/shard_map/all_to_all | solution.py:119
  10.4 93.0 %copy-start.7 = (s32[1,4]{1,0:T(1,128)S(1)}, s32[1,4]{1,0:T(1,128)}, u32[]{:S(2)}) copy-start(s32[1,4]{1,0:T(1,128)} %param.17) | copy-start | bytes 52
  12.3 8.8 %all-to-all-start.1 = ((s32[4,128,1]{1,2,0:T(1,128)}), s32[4,128,1]{1,2,0:T(1,128)S(1)}, u32[]{:S(2)}, u32[]{:S(2)}) async-start(s32[4,128,1]{1,2,0:T(1,128)} %bitcast.18), calls=%async_computation.1 | async-start | bytes 4096 | tf_op jit(solution)/shard_map/all_to_all | solution.py:120
  98.5 10.4 %all-to-all-start.2 = ((s32[8,1,64]{2,1,0:T(1,128)}), s32[8,1,64]{2,1,0:T(1,128)S(1)}, u32[]{:S(2)}, u32[]{:S(2)}) async-start(s32[8,1,64]{2,1,0:T(1,128)} %bitcast.21), calls=%async_computation.2 | async-start | bytes 8192 | tf_op jit(solution)/shard_map/all_to_all | solution.py:94
  103.5 33.6 %copy-start = (f32[512,3,128]{2,0,1:T(8,128)S(1)}, f32[512,3,128]{2,0,1:T(8,128)}, u32[]{:S(2)}) copy-start(f32[512,3,128]{2,0,1:T(8,128)} %param.14) | copy-start | bytes 2359300
  103.5 33.6 %copy-start.1 = (f32[512,3,128]{2,0,1:T(8,128)S(1)}, f32[512,3,128]{2,0,1:T(8,128)}, u32[]{:S(2)}) copy-start(f32[512,3,128]{2,0,1:T(8,128)} %param.13) | copy-start | bytes 2359300
  113.0 9.0 %all-to-all-start.3 = ((f32[8,1,768]{2,1,0:T(1,128)}), f32[8,1,768]{2,1,0:T(1,128)S(1)}, u32[]{:S(2)}, u32[]{:S(2)}) async-start(f32[8,1,768]{2,1,0:T(1,128)} %reshape.593), calls=%async_computation.3 | async-start | bytes 49152 | tf_op jit(solution)/shard_map/all_to_all | solution.py:96
  126.2 11.2 %copy-start.2 = (f32[1,512,128]{2,1,0:T(8,128)S(1)}, f32[1,512,128]{2,1,0:T(8,128)}, u32[]{:S(2)}) copy-start(f32[1,512,128]{2,1,0:T(8,128)} %get-tuple-element.36) | copy-start | bytes 786436
  126.9 8.0 %all-to-all-start.4 = ((f32[12,4,128]{2,0,1:T(8,128)}), f32[12,4,128]{2,0,1:T(8,128)S(1)}, u32[]{:S(2)}, u32[]{:S(2)}) async-start(f32[12,4,128]{2,0,1:T(8,128)} %broadcast_select_fusion), calls=%async_computation.4 | async-start | bytes 65536 | tf_op jit(solution)/shard_map/all_to_all | solution.py:123
  134.9 2.6 %copy-start.3 = (f32[512,128]{1,0:T(8,128)S(1)}, f32[512,128]{1,0:T(8,128)}, u32[]{:S(2)}) copy-start(f32[512,128]{1,0:T(8,128)} %param.11) | copy-start | bytes 786436
  137.1 1.6 %copy-start.4 = (f32[12,512]{1,0:T(8,128)S(1)}, f32[12,512]{1,0:T(8,128)}, u32[]{:S(2)}) copy-start(f32[12,512]{1,0:T(8,128)} %param.20) | copy-start | bytes 73732
  137.3 1.5 %copy-start.5 = (s32[4,512]{1,0:T(4,128)S(1)}, s32[4,512]{1,0:T(4,128)}, u32[]{:S(2)}) copy-start(s32[4,512]{1,0:T(4,128)} %param.18) | copy-start | bytes 24580
  137.3 1.5 %copy-start.6 = (f32[4,512]{1,0:T(4,128)S(1)}, f32[4,512]{1,0:T(4,128)}, u32[]{:S(2)}) copy-start(f32[4,512]{1,0:T(4,128)} %param.19) | copy-start | bytes 24580
where the time goes:
time: 149 us; the launch traced here: 147 us
  local copies, waits for them, and re-layouts  93.4 us (63%)
  starting transfers between devices  20.9 us (14%)
  other arithmetic  16 us (11%)
  waiting for transfers between devices  16 us (11%)
    scatter x1, local copies, waits for them, and re-layouts, lookup(): table = jnp.zeros((peers, width), jnp.int32).at[owner, position].set(offset)  76.9 us
    all_to_all x1, waiting for transfers between devices, lookup(): lax.all_to_all(found, 'dev', split_axis=1, concat_axis=1, tiled=True)  5.68 us
    reduce_sum x1, other arithmetic, master_terms(): jnp.sum(paired * normals[:, direction][None, None], axis=-1).reshape(16, -1)  5.61 us
    all_to_all x1, starting transfers between devices, local(): lax.all_to_all(owner_ids, 'zone', split_axis=0, concat_axis=0, tiled=True)  5.18 us
    all_to_all x1, starting transfers between devices, lookup(): lax.all_to_all(table, 'dev', split_axis=0, concat_axis=0, tiled=True)  4.88 us
    all_to_all x1, waiting for transfers between devices, local(): lax.all_to_all(found, 'zone', split_axis=1, concat_axis=1, tiled=True)  4.71 us
    unnamed x19, local copies, waits for them, and re-layouts  4.45 us
    all_to_all x1, starting transfers between devices, local(): lax.all_to_all(block_patch, 'zone', split_axis=0, concat_axis=0, tiled=True)  4.19 us
  transfers between devices with their start and end apart: 5, of which 4 were waited for; matrix products, arithmetic and copies ran while one was open for 7% of the time, Pallas kernels for 0%

commit v1 on v0

--- a/solution.py
+++ b/solution.py
@@ -76,26 +76,36 @@
     return index % cap < per_slot
 
 
-def lookup(owner, offset, master_patch):
+def lookup(owner, patch, master_patch):
     count = owner.shape[0]
     peers = lax.axis_size("dev")
-    sources = lax.axis_size("zone")
-    width = sources * BUCKET
-    block = count // sources
-    peer_index = jnp.arange(peers, dtype=jnp.int32)
-    hits = (owner.reshape(sources, block)[:, :, None] == peer_index[None, None, :]).astype(
-        jnp.int32
+    zones = lax.axis_size("zone")
+    block = count // zones
+    width = peers * BUCKET
+    owner = owner.reshape(zones, block)
+    patch = patch.reshape(zones, block)
+    index = jnp.arange(block, dtype=jnp.int32)
+    earlier = index[:, None] < index[None, :]
+    same = (owner[:, :, None] == owner[:, None, :]) & earlier[None]
+    rank = jnp.sum(same.astype(jnp.int32), axis=1)
+    place = owner * BUCKET + rank
+    chosen = place[:, :, None] == jnp.arange(width, dtype=jnp.int32)[None, None, :]
+    table = jnp.sum(jnp.where(chosen, patch[:, :, None], 0), axis=1)
+    asked = lax.all_to_all(
+        table.reshape(zones * peers, BUCKET), ("zone", "dev"), split_axis=0, concat_axis=0, tiled=True
     )
-    before = jnp.cumsum(hits, axis=1) - hits
-    rank = jnp.sum(before * hits, axis=2)
-    position = (jnp.arange(sources, dtype=jnp.int32)[:, None] * BUCKET + rank).reshape(count)
-    table = jnp.zeros((peers, width), jnp.int32).at[owner, position].set(offset)
-    found = jnp.take(
-        master_patch, lax.all_to_all(table, "dev", split_axis=0, concat_axis=0, tiled=True), axis=1
+    found = jnp.take(master_patch.T, asked.reshape(-1), axis=0, mode="clip")
+    replies = lax.all_to_all(
+        found.reshape(zones * peers, BUCKET * 12), ("zone", "dev"), split_axis=0, concat_axis=0, tiled=True
     )
-    replies = lax.all_to_all(found, "dev", split_axis=1, concat_axis=1, tiled=True)
-    flat = replies.reshape(12, peers * width)
-    return jnp.take(flat, owner * width + position, axis=1)
+    rows = replies.reshape(zones, width, 12)
+    corners = lax.dot_general(
+        rows,
+        chosen.astype(jnp.float32),
+        (((1,), (2,)), ((0,), (0,))),
+        precision=lax.Precision.HIGHEST,
+    )
+    return corners.transpose(1, 0, 2).reshape(12, count)
 
 
 def local(
@@ -115,12 +125,7 @@
     slots = quad_weight.shape[0]
     mortar_d = slave_terms(quad_weight, param_coords)
     owner_ids = block_owner[:, 0]
-    asked_owner, asked_patch = (
-        lax.all_to_all(owner_ids, "zone", split_axis=0, concat_axis=0, tiled=True),
-        lax.all_to_all(block_patch, "zone", split_axis=0, concat_axis=0, tiled=True),
-    )
-    found = lookup(asked_owner, asked_patch, master_patch)
-    corners = lax.all_to_all(found, "zone", split_axis=1, concat_axis=1, tiled=True)
+    corners = lookup(owner_ids, block_patch, master_patch)
     back_m, back_gap, back_slip, back_lin = master_terms(
         quad_weight, param_coords, slave_points, slave_normals, corners
     )

time: 149 us -> 52.2 us (0.35); the launches traced: 147 us -> 51.9 us
  local copies, waits for them, and re-layouts: 93.4 us -> 13.1 us
  waiting for transfers between devices: 16 us -> 7.23 us
  starting transfers between devices: 20.9 us -> 13.1 us
    scatter x1 -> x0, local copies, waits for them, and re-layouts: 76.9 us -> none  [lookup(): table = jnp.zeros((peers, width), jnp.int32).at[owner, position].set(offset)]
    all_to_all x5 -> x2, waiting for transfers between devices: 16 us -> 7.23 us  [the longest x1 7.23 us: lookup(): lax.all_to_all(found.reshape(zones * peers, BUCKET * 12), ('zone', 'dev')...]
    all_to_all x5 -> x2, starting transfers between devices: 20.9 us -> 13.1 us  [the longest x1 7.3 us: lookup(): lax.all_to_all(table.reshape(zones * peers, BUCKET), ('zone', 'dev'), spl...]
    gather x4 -> x1, local copies, waits for them, and re-layouts: 6.06 us -> 3.22 us  [lookup(): found = jnp.take(master_patch.T, asked.reshape(-1), axis=0, mode='clip')]
    unnamed x19, local copies, waits for them, and re-layouts: 4.45 us -> 2.66 us
    reduce_sum x1 -> x2, other arithmetic: 0.24 us -> 1.8 us  [the longest x1 0.9 us: lookup(): rank = jnp.sum(same.astype(jnp.int32), axis=1)]
  transfers between devices with their start and end apart: 5 -> 2, of which waited for: 4 -> 1; matrix products, arithmetic and copies ran while one was open for 7% -> 18% of each run, Pallas kernels for 0% -> 0%
where the time goes in v1:
time: 52.2 us; the launch traced here: 51.9 us
  other arithmetic  17.1 us (33%)
  local copies, waits for them, and re-layouts  13.1 us (25%)
  starting transfers between devices  13.1 us (25%)
  waiting for transfers between devices  7.23 us (14%)
  between operations  0.88 us (2%)
    all_to_all x1, starting transfers between devices, lookup(): lax.all_to_all(table.reshape(zones * peers, BUCKET), ('zone', 'dev'), spl...  7.3 us
    all_to_all x1, waiting for transfers between devices, lookup(): lax.all_to_all(found.reshape(zones * peers, BUCKET * 12), ('zone', 'dev')...  7.23 us
    all_to_all x1, starting transfers between devices, lookup(): lax.all_to_all(found.reshape(zones * peers, BUCKET * 12), ('zone', 'dev')...  5.83 us
    reduce_sum x1, other arithmetic, master_terms(): jnp.sum(paired * normals[:, direction][None, None], axis=-1).reshape(16, -1)  5.61 us
    slice x1, local copies, waits for them, and re-layouts, slave_terms(): shape_s = bilinear(coords[:, 2], coords[:, 3])  3.67 us
    gather x1, local copies, waits for them, and re-layouts, lookup(): found = jnp.take(master_patch.T, asked.reshape(-1), axis=0, mode='clip')  3.22 us
    unnamed x19, local copies, waits for them, and re-layouts  2.66 us
    reduce_sum x1, other arithmetic, master_terms(): jnp.sum(shape_m * corners[4 * direction:4 * direction + 4][:, :, None], a...  2.15 us
  transfers between devices with their start and end apart: 2, of which 1 were waited for; matrix products, arithmetic and copies ran while one was open for 18% of the time, Pallas kernels for 0%

profile of v1, /device:TPU:0, one launch (start us, length us, event | category | flops | bytes accessed | tf_op | source)
XLA Modules:
  0.0 51.9 jit_solution(12819203930487158303)
XLA Ops:
  0.7 0.9 %convert_reduce_fusion = s32[4,128]{1,0:T(4,128)S(1)} fusion(s32[4,128]{1,0:T(4,128)} %bitcast.81, pred[128,128]{1,0:T(8,128)(4,1)S(1)} %iota_compare_fusion.2), kind=kLoop, calls=%fused_computation.29 | loop fusion | flops 261632 | bytes 20480 | tf_op jit(solution)/shard_map/reduce_sum | solution.py:90
  1.6 0.7 %multiply_add_fusion.1 = s32[4,128]{1,0:T(4,128)S(1)} fusion(s32[4,128]{1,0:T(4,128)S(1)} %convert_reduce_fusion, s32[4,128]{1,0:T(4,128)} %bitcast.82), kind=kLoop, calls=%fused_computation.76 | loop fusion | flops 1024 | bytes 6144 | tf_op jit(solution)/shard_map/add | solution.py:91
  2.3 0.9 %select_reduce_fusion = s32[4,128]{1,0:T(4,128)S(1)} fusion(s32[4,128]{1,0:T(4,128)} %bitcast.83, s32[4,128]{1,0:T(4,128)S(1)} %multiply_add_fusion.1), kind=kLoop, calls=%fused_computation.27 | loop fusion | flops 196096 | bytes 6144 | tf_op jit(solution)/shard_map/reduce_sum | solution.py:93
  3.2 0.7 %all_to_all.12 = s32[32,1,16]{2,0,1:T(8,128)} reshape(s32[4,128]{1,0:T(4,128)S(1)} %select_reduce_fusion) | data formatting | bytes 4096 | tf_op jit(solution)/shard_map/all_to_all | solution.py:94
  3.9 7.3 %all-to-all-start = ((s32[32,1,16]{2,1,0:T(1,128)}), s32[32,1,16]{2,1,0:T(1,128)S(1)}, u32[]{:S(2)}, u32[]{:S(2)}) async-start(s32[32,1,16]{2,1,0:T(1,128)} %bitcast.15), calls=%async_computation | async-start | bytes 32768 | tf_op jit(solution)/shard_map/all_to_all | solution.py:94
  11.2 3.7 %fusion.15 = (f32[512,1,128]{2,1,0:T(1,128)S(1)}, f32[512,1,128]{2,1,0:T(1,128)S(1)}, f32[512,1,128]{2,1,0:T(1,128)S(1)}, f32[512,1,128]{2,1,0:T(1,128)S(1)}) fusion(f32[512,4,128]{2,1,0:T(4,128)} %param.12), kind=kLoop, calls=%fused_computation.82 | loop fusion | bytes 2097152 | tf_op jit(solution)/shard_map/slice | solution.py:26
  14.8 1.2 %slice_bitcast_fusion.1 = (f32[512,128]{1,0:T(8,128)S(1)}, f32[512,128]{1,0:T(8,128)S(1)}, f32[512,128]{1,0:T(8,128)S(1)}) fusion(f32[512,3,128]{2,0,1:T(8,128)} %param.14), kind=kLoop, calls=%fused_computation.31 | loop fusion | bytes 1572864 | tf_op jit(solution)/shard_map/mul | solution.py:48
  16.0 1.1 %multiply_bitcast_fusion.3 = (f32[1,512,128]{2,1,0:T(8,128)}, f32[1,512,128]{2,1,0:T(8,128)}, f32[1,512,128]{2,1,0:T(8,128)}, f32[1,512,128]{2,1,0:T(8,128)}) fusion(f32[512,1,128]{2,0,1:T(8,128)S(1)} %bitcast.80, f32[512,1,128]{2,0,1:T(8,128)S(1)} %bitcast.79), kind=kLoop, calls=%fused_computation.37 | loop fusion | flops 655360 | bytes 1572864 | tf_op jit(solution)/shard_map/mul | solution.py:16
  17.1 0.8 %multiply_bitcast_fusion.7 = (f32[1,512,128]{2,1,0:T(8,128)S(1)}, f32[1,512,128]{2,1,0:T(8,128)S(1)}, f32[1,512,128]{2,1,0:T(8,128)S(1)}, f32[1,512,128]{2,1,0:T(8,128)}) fusion(f32[512,1,128]{2,0,1:T(8,128)S(1)} %bitcast.78, f32[512,1,128]{2,0,1:T(8,128)S(1)} %bitcast.77), kind=kLoop, calls=%fused_computation.43 | loop fusion | flops 655360 | bytes 1572864 | tf_op jit(solution)/shard_map/mul | solution.py:16
  17.9 0.1 select_reduce_fusion.1
  18.0 2.6 %copy.59 = f32[12,8192]{0,1:T(8,128)} copy(f32[12,8192]{1,0:T(8,128)S(1)} %copy-done.3) | data formatting | bytes 786432 | tf_op args[10]
  20.6 0.5 broadcast.272
  21.1 0.7 %reduce.4 = s32[32,16]{1,0:T(8,128)S(1)} reduce(s32[32,1,16]{2,1,0:T(1,128)S(1)} %all-to-all-done, s32[]{:T(128)} %broadcast.272), dimensions={1}, to_apply=%all_to_all.13.reduce_sub_computation.3 | reduce | bytes 4100 | tf_op jit(solution)/shard_map/all_to_all | solution.py:94
  21.8 0.1 reshape.454
  21.9 3.2 %gather_fusion = f32[512,12]{1,0:T(8,128)S(1)} fusion(f32[8192,12]{1,0:T(8,128)} %bitcast.76, s32[1024]{0:T(1024)S(1)} %pad_clamp_fusion), kind=kCustom, calls=%fused_computation | custom fusion | bytes 51200 | tf_op jit(solution)/shard_map/jit(_take)/gather | solution.py:97
  25.1 0.8 %all_to_all.16 = f32[32,1,192]{2,1,0:T(1,128)} reshape(f32[512,12]{1,0:T(8,128)S(1)} %gather_fusion) | data formatting | bytes 49152 | tf_op jit(solution)/shard_map/all_to_all | solution.py:98
  25.9 5.8 %all-to-all-start.1 = ((f32[32,1,192]{2,1,0:T(1,128)}), f32[32,1,192]{2,1,0:T(1,128)S(1)}, u32[]{:S(2)}, u32[]{:S(2)}) async-start(f32[32,1,192]{2,1,0:T(1,128)} %all_to_all.16), calls=%async_computation.1 | async-start | bytes 65536 | tf_op jit(solution)/shard_map/all_to_all | solution.py:98
  31.8 7.2 %all-to-all-done.1 = f32[32,1,192]{2,1,0:T(1,128)S(1)} async-done(((f32[32,1,192]{2,1,0:T(1,128)}), f32[32,1,192]{2,1,0:T(1,128)S(1)}, u32[]{:S(2)}, u32[]{:S(2)}) %all-to-all-start.1) | async-done | bytes 24608 | tf_op jit(solution)/shard_map/all_to_all | solution.py:98
  39.0 0.1 reduce.1
  39.1 0.2 reshape.451
  39.3 0.0 copy-start.4
  39.3 0.4 convolution_bitcast_fusion
  39.8 2.1 %multiply_reduce_fusion.6 = (f32[512,128]{1,0:T(8,128)S(1)}, f32[512,128]{1,0:T(8,128)S(1)}, f32[512,128]{1,0:T(8,128)S(1)}, f32[4,512,128]{2,1,0:T(8,128)S(1)}) fusion(f32[4,512]{1,0:T(4,128)S(1)} %get-tuple-element.40, f32[1,512,128]{2,1,0:T(8,128)} %get-tuple-element.37, f32[1,512,128]{2,1,0:T(8,128)} %get-tuple-element.38, ...), kind=kLoop, calls=%fused_computation.16 | loop fusion | flops 2162688 | bytes 2908160 | tf_op jit(solution)/shard_map/reduce_sum | solution.py:39
  41.9 0.0 copy-start.5
  41.9 0.2 multiply_subtract_fusion.1
  42.1 0.1 multiply_subtract_fusion
  42.3 1.3 %multiply_reduce_fusion.4 = (f32[4,512]{1,0:T(4,128)S(1)}, f32[4,512]{1,0:T(4,128)S(1)}, f32[4,512]{1,0:T(4,128)S(1)}, f32[4,512]{1,0:T(4,128)S(1)}, f32[4,512,128]{2,1,0:T(8,128)S(1)}, /*index=5*/f32[4,512,128]{2,1,0:T(8,128)S(1)}) fusion(f32[512,128]{1,0:T(8,128)S(1)} %get-tuple-element.21, f32[512,128]{1,0:T(8,128)S(1)} %get-tuple-element.20, ...), kind=kLoop, calls=%fused_computation.14 | loop fusion | flops 3137536 | bytes 4489216 | tf_op jit(solution)/shard_map/reduce_sum | solution.py:44
  43.6 0.6 %maximum_divide_fusion = (f32[4,512]{1,0:T(4,128)S(1)}, f32[4,512]{1,0:T(4,128)}) fusion(f32[12,512]{1,0:T(8,128)S(1)} %fusion.5, f32[4,512]{1,0:T(4,128)S(1)} %copy-done.7, f32[4,512]{1,0:T(4,128)S(1)} %get-tuple-element.12, s32[4,512]{1,0:T(4,128)S(1)} %copy-done.6, pred[512]{0:T(512)(128)(4,1)S(1)} %fusion.9), kind=kLoop, calls=%fused_computation.56 | loop fusion | flops 22528 | bytes 66048 | tf_op jit(solution)/shard_map/div | solution.py:58
  44.2 0.6 %fusion.4 = f32[12,512]{1,0:T(8,128)} fusion(f32[12,512]{1,0:T(8,128)S(1)} %copy-done.5, f32[4,512]{1,0:T(4,128)S(1)} %get-tuple-element.42, s32[4,512]{1,0:T(4,128)S(1)} %copy-done.6, pred[512]{0:T(512)(128)(4,1)S(1)} %fusion.9, f32[4,512]{1,0:T(4,128)S(1)} %get-tuple-element.10, f32[4,512]{1,0:T(4,128)S(1)} %get-tuple-element.11, ...), kind=kLoop, calls=%fused_computation.49 | loop fusion | flops 79872 | bytes 90624 | tf_op jit(solution)/shard_map/jit(_where)/select_n | solution.py:139
  44.9 5.6 %fusion = (f32[4,4,512]{2,1,0:T(4,128)S(1)}, f32[4,4,512]{2,1,0:T(4,128)S(1)}, f32[4,4,512]{2,1,0:T(4,128)S(1)}, f32[4,4,512]{2,1,0:T(4,128)S(1)}, f32[4,4,512]{2,1,0:T(4,128)S(1)}) fusion(f32[512,128]{1,0:T(8,128)S(1)} %get-tuple-element.29, f32[4,512,128]{2,1,0:T(8,128)S(1)} %get-tuple-element.27, f32[4,512,128]{2,1,0:T(8,128)S(1)} %get-tuple-element.17, ...), kind=kLoop, calls=%fused_computation.5 | loop fusion | flops 10444800 | bytes 4096000 | tf_op jit(solution)/shard_map/reduce_sum | solution.py:48
  50.6 0.6 %broadcast_select_fusion = (f32[16,512]{1,0:T(8,128)}, f32[16,512]{1,0:T(8,128)}) fusion(f32[16,512]{1,0:T(8,128)S(1)} %reshape.447, pred[512]{0:T(512)(128)(4,1)S(1)} %fusion.9, f32[16,512]{1,0:T(8,128)S(1)} %reshape.446), kind=kLoop, calls=%fused_computation.54 | loop fusion | flops 16384 | bytes 131584 | tf_op jit(solution)/shard_map/jit(_where)/select_n | solution.py:136
  51.2 0.6 %maximum_select_fusion = f32[48,512]{1,0:T(8,128)} fusion(f32[16,512]{1,0:T(8,128)S(1)} %reshape.450, f32[16,512]{1,0:T(8,128)S(1)} %reshape.449, f32[16,512]{1,0:T(8,128)S(1)} %reshape.448, pred[512]{0:T(512)(128)(4,1)S(1)} %fusion.9), kind=kLoop, calls=%fused_computation.46 | loop fusion | flops 73728 | bytes 197120 | tf_op jit(solution)/shard_map/jit(_where)/select_n | solution.py:137
  (28 shorter events, 0.2 us)
Async XLA Ops:
  0.6 17.2 %copy-start.8 = (s32[1,4]{1,0:T(1,128)S(1)}, s32[1,4]{1,0:T(1,128)}, u32[]{:S(2)}) copy-start(s32[1,4]{1,0:T(1,128)} %param.17) | copy-start | bytes 52
  0.6 17.3 %copy-start.3 = (f32[12,8192]{1,0:T(8,128)S(1)}, f32[12,8192]{1,0:T(8,128)}, u32[]{:S(2)}) copy-start(f32[12,8192]{1,0:T(8,128)} %param.21) | copy-start | bytes 1179652
  3.9 16.7 %all-to-all-start = ((s32[32,1,16]{2,1,0:T(1,128)}), s32[32,1,16]{2,1,0:T(1,128)S(1)}, u32[]{:S(2)}, u32[]{:S(2)}) async-start(s32[32,1,16]{2,1,0:T(1,128)} %bitcast.15), calls=%async_computation | async-start | bytes 32768 | tf_op jit(solution)/shard_map/all_to_all | solution.py:94
  20.6 21.3 %copy-start = (f32[512,3,128]{2,0,1:T(8,128)S(1)}, f32[512,3,128]{2,0,1:T(8,128)}, u32[]{:S(2)}) copy-start(f32[512,3,128]{2,0,1:T(8,128)} %param.14) | copy-start | bytes 2359300
  20.6 21.3 %copy-start.1 = (f32[512,3,128]{2,0,1:T(8,128)S(1)}, f32[512,3,128]{2,0,1:T(8,128)}, u32[]{:S(2)}) copy-start(f32[512,3,128]{2,0,1:T(8,128)} %param.13) | copy-start | bytes 2359300
  25.9 13.1 %all-to-all-start.1 = ((f32[32,1,192]{2,1,0:T(1,128)}), f32[32,1,192]{2,1,0:T(1,128)S(1)}, u32[]{:S(2)}, u32[]{:S(2)}) async-start(f32[32,1,192]{2,1,0:T(1,128)} %all_to_all.16), calls=%async_computation.1 | async-start | bytes 65536 | tf_op jit(solution)/shard_map/all_to_all | solution.py:98
  39.3 3.0 %copy-start.2 = (f32[1,512,128]{2,1,0:T(8,128)S(1)}, f32[1,512,128]{2,1,0:T(8,128)}, u32[]{:S(2)}) copy-start(f32[1,512,128]{2,1,0:T(8,128)} %get-tuple-element.34) | copy-start | bytes 786436
  39.3 3.0 %copy-start.4 = (f32[512,128]{1,0:T(8,128)S(1)}, f32[512,128]{1,0:T(8,128)}, u32[]{:S(2)}) copy-start(f32[512,128]{1,0:T(8,128)} %param.11) | copy-start | bytes 786436
  41.9 1.6 %copy-start.5 = (f32[12,512]{1,0:T(8,128)S(1)}, f32[12,512]{1,0:T(8,128)}, u32[]{:S(2)}) copy-start(f32[12,512]{1,0:T(8,128)} %param.20) | copy-start | bytes 73732
  42.1 1.5 %copy-start.6 = (s32[4,512]{1,0:T(4,128)S(1)}, s32[4,512]{1,0:T(4,128)}, u32[]{:S(2)}) copy-start(s32[4,512]{1,0:T(4,128)} %param.18) | copy-start | bytes 24580
  42.1 1.5 %copy-start.7 = (f32[4,512]{1,0:T(4,128)S(1)}, f32[4,512]{1,0:T(4,128)}, u32[]{:S(2)}) copy-start(f32[4,512]{1,0:T(4,128)} %param.19) | copy-start | bytes 24580

commit v2 on v0

v2 whole, which is shorter than its diff:
```python
import functools

import jax
import jax.numpy as jnp
from jax import lax
from jax.experimental import pallas as pl
from jax.experimental.pallas import tpu as pltpu
from jax.sharding import PartitionSpec as P

BUCKET = 16
LANES = 128
MESH = pl.DeviceIdType.MESH

friction_coef = 0.3
newton_scale = 4.0


def pick(values, index, axis):
    return jnp.take_along_axis(values, index, axis=axis, mode="promise_in_bounds")


def iota(shape, axis):
    return lax.broadcasted_iota(jnp.int32, shape, axis)


def bilinear(first, second):
    return (
        0.25 * (1.0 - first) * (1.0 - second),
        0.25 * (1.0 + first) * (1.0 - second),
        0.25 * (1.0 + first) * (1.0 + second),
        0.25 * (1.0 - first) * (1.0 + second),
    )


NS, NM, WS, PT, NV = 0, 4, 8, 12, 15


def kernel(
    zones,
    peers,
    quad_hbm,
    coords_hbm,
    points_hbm,
    normals_hbm,
    master_hbm,
    owner_ref,
    patch_ref,
    count_ref,
    active_ref,
    nmult_ref,
    tmult_ref,
    d_ref,
    m_ref,
    lin_ref,
    gap_ref,
    cone_ref,
    quad,
    coords,
    points,
    normals,
    table,
    packed,
    terms,
    req_out,
    req_in,
    rep_out,
    rep_in,
    load_sem,
    req_send,
    req_recv,
    rep_send,
    rep_recv,
):
    count = zones * peers
    groups = peers // 8
    zone, dev = lax.axis_index("zone"), lax.axis_index("dev")
    me = zone * peers + dev
    tiles = table.shape[1] // LANES
    half = tiles // 2

    loads = [
        pltpu.make_async_copy(source, target, load_sem.at[at])
        for at, (source, target) in enumerate(
            (
                (master_hbm, table),
                (quad_hbm, quad),
                (coords_hbm, coords),
                (points_hbm, points),
                (normals_hbm, normals),
            )
        )
    ]
    for load in loads:
        load.start()

    barrier = pltpu.get_barrier_semaphore()

    def greet(step, carry):
        other = lax.rem(me + step, count)
        pl.semaphore_signal(
            barrier,
            inc=1,
            device_id=(lax.div(other, peers), lax.rem(other, peers)),
            device_id_type=MESH,
        )
        return carry

    lax.fori_loop(1, count, greet, 0)

    sub, lane = iota((8, LANES), 0), iota((8, LANES), 1)
    wide_sub, wide_lane = iota((LANES, LANES), 0), iota((LANES, LANES), 1)
    ranks = []
    for k in range(zones):
        owner = owner_ref[k : k + 1, :].astype(jnp.float32)
        patch = patch_ref[k : k + 1, :].astype(jnp.float32)
        across = jnp.broadcast_to(owner, (LANES, LANES))
        same = (across.T == across) & (wide_sub < wide_lane)
        rank = jnp.sum(jnp.where(same, 1.0, 0.0), axis=0, keepdims=True).astype(jnp.int32)
        ranks.append(rank)
        place = owner_ref[k : k + 1, :] * BUCKET + rank
        for g in range(groups):
            chosen = jnp.where(wide_sub + g * LANES == place, jnp.broadcast_to(patch, (LANES, LANES)), 0.0)
            asked = jnp.sum(chosen.T, axis=0, keepdims=True).astype(jnp.int32)
            rows = pick(jnp.broadcast_to(asked, (8, LANES)), sub * BUCKET + (lane & 15), 1)
            for o in range(8):
                req_out[k * peers + g * 8 + o] = rows[o : o + 1, :]

    pl.semaphore_wait(barrier, count - 1)

    def ask(step, carry):
        other = lax.rem(me + step, count)
        pltpu.make_async_remote_copy(
            src_ref=req_out.at[other],
            dst_ref=req_in.at[me],
            send_sem=req_send,
            recv_sem=req_recv.at[zone],
            device_id=(lax.div(other, peers), lax.rem(other, peers)),
            device_id_type=MESH,
        ).start()
        return carry

    lax.fori_loop(1, count, ask, 0)
    pltpu.make_async_copy(req_out.at[me], req_in.at[me], req_recv.at[zone]).start()

    loads[0].wait()
    packed[0:4, :] = table[8:12, 0 : half * LANES]
    packed[4:8, :] = table[8:12, half * LANES : tiles * LANES]
    for load in loads[1:]:
        load.wait()

    def stage(k, carry):
        rows = pl.ds(pl.multiple_of(k * LANES, LANES), LANES)

        def coord(which):
            return coords[pl.ds(k * (4 * LANES) + which, LANES, stride=4), :].T

        weight = quad[rows, :].T
        shape_s = bilinear(coord(2), coord(3))
        for i in range(4):
            terms[NS + i, k] = shape_s[i]
            terms[WS + i, k] = weight * shape_s[i]
        shape_m = bilinear(coord(0), coord(1))
        for i in range(4):
            terms[NM + i, k] = shape_m[i]
        for c in range(3):
            terms[PT + c, k] = points[c, rows, :].T
            terms[NV + c, k] = normals[c, rows, :].T
        return carry

    lax.fori_loop(0, zones, stage, 0)

    skew = ((lane >> 4) - sub) & 7
    skew_low = ((lane >> 4) - (sub & 3)) & 7
    upper = jnp.where(sub >= 4, half, 0)
    for dz in range(zones):
        target = lax.rem(zone + dz, zones)
        whole = req_in.at[pl.ds(target * peers, peers)]
        pltpu.make_async_copy(whole, whole, req_recv.at[target]).wait()
        for g in range(groups):
            base = target * peers + g * 8
            rows = jnp.concatenate([req_in[base + v] for v in range(8)], axis=0)
            first = pick(rows, skew, 0)
            second = pick(rows, skew_low, 0)
            high, low = first >> 7, first & 127
            high_b, low_b = (second >> 7) - upper, second & 127
            zero = jnp.zeros((8, LANES), jnp.float32)

            def search(h, accs):
                acc, acc_a, acc_b = accs
                at = pl.ds(pl.multiple_of(h * LANES, LANES), LANES)
                later = pl.ds(pl.multiple_of((h + half) * LANES, LANES), LANES)
                acc = jnp.where(high == h, pick(table[0:8, at], low, 1), acc)
                acc_a = jnp.where(high == h + half, pick(table[0:8, later], low, 1), acc_a)
                acc_b = jnp.where(high_b == h, pick(packed[:, at], low_b, 1), acc_b)
                return acc, acc_a, acc_b

            acc, acc_a, acc_b = lax.fori_loop(0, half, search, (zero, zero, zero), unroll=8)
            acc = jnp.where(high >= half, acc_a, acc)
            acc_b = acc_b + pltpu.roll(acc_b, 4, 0)
            out_a, out_b = pick(acc, skew, 0), pick(acc_b, skew, 0)
            for v in range(8):
                rep_out[base + v, :, 0:LANES] = out_a[v : v + 1, :]
                rep_out[base + v, :, LANES : 2 * LANES] = out_b[v : v + 1, :]

        def answer(step, carry):
            peer = lax.rem(dev + step, peers)
            pltpu.make_async_remote_copy(
                src_ref=rep_out.at[target * peers + peer],
                dst_ref=rep_in.at[me],
                send_sem=rep_send,
                recv_sem=rep_recv.at[zone],
                device_id=(target, peer),
                device_id_type=MESH,
            ).start()
            return carry

        if dz == 0:
            pltpu.make_async_copy(rep_out.at[me], rep_in.at[me], rep_recv.at[zone]).start()
        lax.fori_loop(1 if dz == 0 else 0, peers, answer, 0)

    for k in range(zones):
        live = lane[0:1] < count_ref[0, k]
        cols = slice(k * LANES, (k + 1) * LANES)

        def keep(ref, row, value):
            total = jnp.sum(value, axis=0, keepdims=True)
            ref[row : row + 1, cols] = jnp.where(live, total, 0.0)

        for i in range(4):

            def add(t, accs):
                at = pl.ds(pl.multiple_of(t * 8, 8), 8)
                weighted = terms[WS + i, k, at, :]
                normal = [terms[NV + c, k, at, :] for c in range(3)]
                out = [accs[j] + weighted * terms[NS + j, k, at, :] for j in range(4)]
                pairs = [weighted * terms[NM + a, k, at, :] for a in range(4)]
                out += [accs[4 + a] + pairs[a] for a in range(4)]
                out += [accs[8 + c * 4 + a] + pairs[a] * normal[c] for c in range(3) for a in range(4)]
                return tuple(out)

            zero = jnp.zeros((8, LANES), jnp.float32)
            accs = lax.fori_loop(0, LANES // 8, add, (zero,) * 20, unroll=4)
            for j in range(4):
                keep(d_ref, i * 4 + j, accs[j])
                keep(m_ref, i * 4 + j, accs[4 + j])
                for c in range(3):
                    keep(lin_ref, c * 16 + i * 4 + j, accs[8 + c * 4 + j])

    turn = dev & 7
    undo = ((((lane >> 4) - sub) & 7) << 4) + (lane & 15)
    mix = ((lane >> 4) - sub - turn) & 7
    for dz in range(zones):
        k = dz
        whole = rep_in.at[pl.ds(k * peers, peers)]
        pltpu.make_async_copy(whole, whole, rep_recv.at[k]).wait()
        owner = jnp.broadcast_to(owner_ref[k : k + 1, :], (8, LANES))
        seat = (((owner + sub + turn) & 7) << 4) + jnp.broadcast_to(ranks[k], (8, LANES))
        found = []
        for h in range(2):
            total = jnp.zeros((8, LANES), jnp.float32)
            for g in range(groups):
                rows = jnp.concatenate(
                    [
                        rep_in[k * peers + g * 8 + o, :, h * LANES : (h + 1) * LANES]
                        for o in range(8)
                    ],
                    axis=0,
                )
                rows = pick(pick(pick(rows, undo, 1), mix, 0), seat, 1)
                total = jnp.where((owner >> 3) == g, rows, total)
            found.append(total)
        corner = [
            jnp.broadcast_to(found[r // 8][r % 8 : r % 8 + 1, :], (8, LANES)) for r in range(12)
        ]

        def add(t, accs):
            at = pl.ds(pl.multiple_of(t * 8, 8), 8)
            shape_m = [terms[NM + a, k, at, :] for a in range(4)]
            diff, normal = [], [terms[NV + c, k, at, :] for c in range(3)]
            for c in range(3):
                position = shape_m[0] * corner[4 * c]
                for a in range(1, 4):
                    position = position + shape_m[a] * corner[4 * c + a]
                diff.append(position - terms[PT + c, k, at, :])
            gap = normal[0] * diff[0] + normal[1] * diff[1] + normal[2] * diff[2]
            slip = [diff[c] - normal[c] * gap for c in range(3)]
            weighted = [terms[WS + i, k, at, :] for i in range(4)]
            out = [accs[i] + weighted[i] * gap for i in range(4)]
            out += [accs[4 + c * 4 + i] + weighted[i] * slip[c] for c in range(3) for i in range(4)]
            return tuple(out)

        zero = jnp.zeros((8, LANES), jnp.float32)
        accs = lax.fori_loop(0, LANES // 8, add, (zero,) * 16, unroll=2)
        sums = [jnp.sum(acc, axis=0, keepdims=True) for acc in accs]
        cols = slice(k * LANES, (k + 1) * LANES)
        live = lane[0:1] < count_ref[0, k]
        wgap = jnp.concatenate(sums[0:4], axis=0)
        active = active_ref[:, cols] == 1
        normal = nmult_ref[:, cols]
        tangent = [tmult_ref[4 * c : 4 * c + 4, cols] for c in range(3)]
        trial = [
            tangent[c] + newton_scale * jnp.concatenate(sums[4 + 4 * c : 8 + 4 * c], axis=0)
            for c in range(3)
        ]
        radius = friction_coef * normal
        length = jnp.sqrt(trial[0] * trial[0] + trial[1] * trial[1] + trial[2] * trial[2])
        factor = radius / jnp.maximum(radius, length)
        for c in range(3):
            cone = jnp.where(active, tangent[c] - factor * trial[c], tangent[c])
            cone_ref[4 * c : 4 * c + 4, cols] = jnp.where(live, cone, 0.0)
        gap_ref[:, cols] = jnp.where(live, jnp.where(active, wgap, normal), 0.0)

    sent = req_out.at[pl.ds(0, count - 1)]
    pltpu.make_async_copy(sent, sent, req_send).wait()
    sent = rep_out.at[pl.ds(0, count - 1)]
    pltpu.make_async_copy(sent, sent, rep_send).wait()


def local(
    quad_weight,
    param_coords,
    slave_points,
    slave_normals,
    block_owner,
    block_patch,
    block_count,
    active_flags,
    normal_mult,
    tangent_mult,
    master_patch,
):
    zones, peers = lax.axis_size("zone"), lax.axis_size("dev")
    slots, gauss = quad_weight.shape
    block = slots // zones
    patches = master_patch.shape[1]
    count = zones * peers
    f32 = jnp.float32
    anywhere = pl.BlockSpec(memory_space=pl.ANY)
    vmem = pl.BlockSpec(memory_space=pltpu.VMEM)
    smem = pl.BlockSpec(memory_space=pltpu.SMEM)
    out = [jax.ShapeDtypeStruct((rows, slots), f32) for rows in (16, 16, 48, 4, 12)]
    return pl.pallas_call(
        functools.partial(kernel, zones, peers),
        out_shape=out,
        in_specs=[anywhere] * 5 + [vmem, vmem, smem, vmem, vmem, vmem],
        out_specs=[vmem] * 5,
        scratch_shapes=[
            pltpu.VMEM((slots, gauss), f32),
            pltpu.VMEM((4 * slots, gauss), f32),
            pltpu.VMEM((3, slots, gauss), f32),
            pltpu.VMEM((3, slots, gauss), f32),
            pltpu.VMEM((12, patches), f32),
            pltpu.VMEM((8, patches // 2), f32),
            pltpu.VMEM((18, zones, gauss, block), f32),
            pltpu.VMEM((count, 1, LANES), jnp.int32),
            pltpu.VMEM((count, 1, LANES), jnp.int32),
            pltpu.VMEM((count, 1, 2 * LANES), f32),
            pltpu.VMEM((count, 1, 2 * LANES), f32),
            pltpu.SemaphoreType.DMA((5,)),
            pltpu.SemaphoreType.DMA,
            pltpu.SemaphoreType.DMA((zones,)),
            pltpu.SemaphoreType.DMA,
            pltpu.SemaphoreType.DMA((zones,)),
        ],
        compiler_params=pltpu.CompilerParams(
            collective_id=0, has_side_effects=True, vmem_limit_bytes=40 * 2**20
        ),
    )(
        quad_weight,
        param_coords.reshape(4 * slots, gauss),
        slave_points.transpose(1, 0, 2),
        slave_normals.transpose(1, 0, 2),
        master_patch,
        block_owner.reshape(zones, block),
        block_patch.reshape(zones, block),
        block_count,
        active_flags,
        normal_mult,
        tangent_mult,
    )


def solution(mesh):
    rows = P(("zone", "dev"))
    columns = P(None, ("zone", "dev"))
    return jax.shard_map(
        local,
        mesh=mesh,
        in_specs=(rows,) * 7 + (columns,) * 4,
        out_specs=(columns,) * 5,
        check_vma=False,
    )
```

time: 149 us -> 32 us (0.21)
  local copies, waits for them, and re-layouts: 93.4 us -> 12.1 us
  starting transfers between devices: 20.9 us -> 0 us
  Pallas kernels: 0 us -> 18.8 us
  other arithmetic: 16 us -> 0 us
  waiting for transfers between devices: 16 us -> 0 us
    scatter x1 -> x0, local copies, waits for them, and re-layouts: 76.9 us -> none  [lookup(): table = jnp.zeros((peers, width), jnp.int32).at[owner, position].set(offset)]
    all_to_all x5 -> x0, starting transfers between devices: 20.9 us -> none  [the longest x1 5.18 us: local(): lax.all_to_all(owner_ids, 'zone', split_axis=0, concat_axis=0, tiled=True)]
    pallas_call x0 -> x1, Pallas kernels: none -> 18.8 us  [local(): pl.pallas_call(functools.partial(kernel, zones, peers), out_shape=out, in...]
    all_to_all x5 -> x0, waiting for transfers between devices: 16 us -> none  [the longest x1 5.68 us: lookup(): lax.all_to_all(found, 'dev', split_axis=1, concat_axis=1, tiled=True)]
    reduce_sum x5 -> x0, other arithmetic: 9.38 us -> none  [the longest x1 5.61 us: master_terms(): jnp.sum(paired * normals[:, direction][None, None], axis=-1).reshape(16, -1)]
    unnamed x19 -> x27, local copies, waits for them, and re-layouts: 4.45 us -> 12.1 us
    gather x4 -> x0, local copies, waits for them, and re-layouts: 6.06 us -> none  [the longest x2 3.36 us: lookup(): jnp.take(master_patch, lax.all_to_all(table, 'dev', split_axis=0, concat_...]
    slice x1 -> x0, local copies, waits for them, and re-layouts: 3.39 us -> none  [slave_terms(): shape_s = bilinear(coords[:, 2], coords[:, 3])]
  transfers between devices with their start and end apart: 5 -> 0, of which waited for: 4 -> 0; matrix products, arithmetic and copies ran while one was open for 7% -> 0% of each run, Pallas kernels for 0% -> 0%
where the time goes in v2:
time: 32 us; the launch traced here: 31.5 us
  Pallas kernels  18.8 us (59%)
  local copies, waits for them, and re-layouts  12.1 us (38%)
  between operations  0.67 us (2%)
    pallas_call x1, Pallas kernels, local(): pl.pallas_call(functools.partial(kernel, zones, peers), out_shape=out, in...  18.8 us
    unnamed x27, local copies, waits for them, and re-layouts  12.1 us

profile of v2, /device:TPU:0, one launch (start us, length us, event | category | flops | bytes accessed | tf_op | source)
XLA Modules:
  0.0 31.5 jit_solution(14879909138948700121)
XLA Ops:
  0.6 0.0 copy-start.6
  0.6 0.0 copy-start.10
  0.7 0.7 %copy-done.6 = s32[4,512]{1,0:T(4,128)S(1)} copy-done((s32[4,512]{1,0:T(4,128)S(1)}, s32[4,512]{1,0:T(4,128)}, u32[]{:S(2)}) %copy-start.6) | copy-done | bytes 8216
  1.3 0.0 copy-done.10
  1.3 0.0 copy-start
  1.3 1.2 %copy-done = f32[512,4,128]{2,1,0:T(4,128)S(1)} copy-done((f32[512,4,128]{2,1,0:T(4,128)S(1)}, f32[512,4,128]{2,1,0:T(4,128)}, u32[]{:S(2)}) %copy-start) | copy-done | bytes 1048600
  2.6 0.0 copy-start.1
  2.6 1.1 %copy-done.1 = f32[512,3,128]{2,0,1:T(8,128)S(1)} copy-done((f32[512,3,128]{2,0,1:T(8,128)S(1)}, f32[512,3,128]{2,0,1:T(8,128)}, u32[]{:S(2)}) %copy-start.1) | copy-done | bytes 786456
  3.7 0.0 copy-start.2
  3.7 1.1 %copy-done.2 = f32[512,3,128]{2,0,1:T(8,128)S(1)} copy-done((f32[512,3,128]{2,0,1:T(8,128)S(1)}, f32[512,3,128]{2,0,1:T(8,128)}, u32[]{:S(2)}) %copy-start.2) | copy-done | bytes 786456
  4.8 0.0 copy-start.3
  4.8 1.0 %copy-done.3 = f32[12,8192]{1,0:T(8,128)S(1)} copy-done((f32[12,8192]{1,0:T(8,128)S(1)}, f32[12,8192]{1,0:T(8,128)}, u32[]{:S(2)}) %copy-start.3) | copy-done | bytes 393240
  5.9 0.0 copy-start.4
  5.9 0.9 %copy-done.4 = f32[512,128]{1,0:T(8,128)S(1)} copy-done((f32[512,128]{1,0:T(8,128)S(1)}, f32[512,128]{1,0:T(8,128)}, u32[]{:S(2)}) %copy-start.4) | copy-done | bytes 262168
  6.8 0.0 copy-start.5
  6.8 0.8 %copy-done.5 = f32[12,512]{1,0:T(8,128)S(1)} copy-done((f32[12,512]{1,0:T(8,128)S(1)}, f32[12,512]{1,0:T(8,128)}, u32[]{:S(2)}) %copy-start.5) | copy-done | bytes 24600
  7.6 0.0 copy-start.7
  7.6 0.7 %copy-done.7 = f32[4,512]{1,0:T(4,128)S(1)} copy-done((f32[4,512]{1,0:T(4,128)S(1)}, f32[4,512]{1,0:T(4,128)}, u32[]{:S(2)}) %copy-start.7) | copy-done | bytes 8216
  8.3 0.0 copy-start.8
  8.3 0.7 %copy-done.8 = s32[512,1]{0,1:T(1,128)S(1)} copy-done((s32[512,1]{0,1:T(1,128)S(1)}, s32[512,1]{0,1:T(1,128)}, u32[]{:S(2)}) %copy-start.8) | copy-done | bytes 2072
  9.0 0.0 copy-start.9
  9.0 0.7 %copy-done.9 = s32[512]{0:T(512)S(1)} copy-done((s32[512]{0:T(512)S(1)}, s32[512]{0:T(512)}, u32[]{:S(2)}) %copy-start.9) | copy-done | bytes 2072
  9.6 18.8 %shard_map.146 = (f32[16,512]{1,0:T(8,128)S(1)}, f32[16,512]{1,0:T(8,128)S(1)}, f32[48,512]{1,0:T(8,128)S(1)}, f32[4,512]{1,0:T(4,128)S(1)}, f32[12,512]{1,0:T(8,128)S(1)}) custom-call(f32[512,128]{1,0:T(8,128)S(1)} %copy-done.4, f32[2048,128]{1,0:T(8,128)S(1)} %bitcast.5, f32[3,512,128]{2,1,0:T(8,128)S(1)} %bitcast.6, f32[3,512,128]{2,1,0:T(8,128)S(1)} %bitcast.7, ...), custom_call_target="tpu_custom_call" | custom-call | tf_op jit(solution)/shard_map/pallas_call | solution.py:342
  28.4 0.6 %copy.21 = f32[16,512]{1,0:T(8,128)} copy(f32[16,512]{1,0:T(8,128)S(1)} %get-tuple-element.10) | data formatting | bytes 65536
  29.0 0.6 %copy.22 = f32[16,512]{1,0:T(8,128)} copy(f32[16,512]{1,0:T(8,128)S(1)} %get-tuple-element.11) | data formatting | bytes 65536
  29.7 0.6 %copy.23 = f32[48,512]{1,0:T(8,128)} copy(f32[48,512]{1,0:T(8,128)S(1)} %get-tuple-element.12) | data formatting | bytes 196608
  30.3 0.6 %copy.24 = f32[4,512]{1,0:T(4,128)} copy(f32[4,512]{1,0:T(4,128)S(1)} %get-tuple-element.13) | data formatting | bytes 16384
  30.9 0.6 %copy.25 = f32[12,512]{1,0:T(8,128)} copy(f32[12,512]{1,0:T(8,128)S(1)} %get-tuple-element.14) | data formatting | bytes 49152
Async XLA Ops:
  0.6 0.7 %copy-start.6 = (s32[4,512]{1,0:T(4,128)S(1)}, s32[4,512]{1,0:T(4,128)}, u32[]{:S(2)}) copy-start(s32[4,512]{1,0:T(4,128)} %active_ref.1) | copy-start | bytes 24580
  0.6 0.7 %copy-start.10 = (s32[1,4]{1,0:T(1,128)S(1)}, s32[1,4]{1,0:T(1,128)}, u32[]{:S(2)}) copy-start(s32[1,4]{1,0:T(1,128)} %count_ref.1) | copy-start | bytes 52
  1.3 1.2 %copy-start = (f32[512,4,128]{2,1,0:T(4,128)S(1)}, f32[512,4,128]{2,1,0:T(4,128)}, u32[]{:S(2)}) copy-start(f32[512,4,128]{2,1,0:T(4,128)} %param.12) | copy-start | bytes 3145732
  2.6 1.1 %copy-start.1 = (f32[512,3,128]{2,0,1:T(8,128)S(1)}, f32[512,3,128]{2,0,1:T(8,128)}, u32[]{:S(2)}) copy-start(f32[512,3,128]{2,0,1:T(8,128)} %param.13) | copy-start | bytes 2359300
  3.7 1.1 %copy-start.2 = (f32[512,3,128]{2,0,1:T(8,128)S(1)}, f32[512,3,128]{2,0,1:T(8,128)}, u32[]{:S(2)}) copy-start(f32[512,3,128]{2,0,1:T(8,128)} %param.14) | copy-start | bytes 2359300
  4.8 1.0 %copy-start.3 = (f32[12,8192]{1,0:T(8,128)S(1)}, f32[12,8192]{1,0:T(8,128)}, u32[]{:S(2)}) copy-start(f32[12,8192]{1,0:T(8,128)} %master_hbm.1) | copy-start | bytes 1179652
  5.9 0.9 %copy-start.4 = (f32[512,128]{1,0:T(8,128)S(1)}, f32[512,128]{1,0:T(8,128)}, u32[]{:S(2)}) copy-start(f32[512,128]{1,0:T(8,128)} %quad_hbm.1) | copy-start | bytes 786436
  6.8 0.8 %copy-start.5 = (f32[12,512]{1,0:T(8,128)S(1)}, f32[12,512]{1,0:T(8,128)}, u32[]{:S(2)}) copy-start(f32[12,512]{1,0:T(8,128)} %tmult_ref.1) | copy-start | bytes 73732
  7.6 0.7 %copy-start.7 = (f32[4,512]{1,0:T(4,128)S(1)}, f32[4,512]{1,0:T(4,128)}, u32[]{:S(2)}) copy-start(f32[4,512]{1,0:T(4,128)} %nmult_ref.1) | copy-start | bytes 24580
  8.3 0.7 %copy-start.8 = (s32[512,1]{0,1:T(1,128)S(1)}, s32[512,1]{0,1:T(1,128)}, u32[]{:S(2)}) copy-start(s32[512,1]{0,1:T(1,128)} %param.15) | copy-start | bytes 6148
  9.0 0.7 %copy-start.9 = (s32[512]{0:T(512)S(1)}, s32[512]{0:T(512)}, u32[]{:S(2)}) copy-start(s32[512]{0:T(512)} %param.16) | copy-start | bytes 6148

commit v3 on v2

--- a/solution.py
+++ b/solution.py
@@ -43,12 +43,12 @@
     points_hbm,
     normals_hbm,
     master_hbm,
-    owner_ref,
-    patch_ref,
-    count_ref,
-    active_ref,
-    nmult_ref,
-    tmult_ref,
+    owner_hbm,
+    patch_hbm,
+    count_hbm,
+    active_hbm,
+    nmult_hbm,
+    tmult_hbm,
     d_ref,
     m_ref,
     lin_ref,
@@ -60,6 +60,12 @@
     normals,
     table,
     packed,
+    owner_ref,
+    patch_ref,
+    count_ref,
+    active_ref,
+    nmult_ref,
+    tmult_ref,
     terms,
     req_out,
     req_in,
@@ -82,11 +88,17 @@
         pltpu.make_async_copy(source, target, load_sem.at[at])
         for at, (source, target) in enumerate(
             (
+                (owner_hbm, owner_ref),
+                (patch_hbm, patch_ref),
                 (master_hbm, table),
                 (quad_hbm, quad),
                 (coords_hbm, coords),
                 (points_hbm, points),
                 (normals_hbm, normals),
+                (count_hbm, count_ref),
+                (active_hbm, active_ref),
+                (nmult_hbm, nmult_ref),
+                (tmult_hbm, tmult_ref),
             )
         )
     ]
@@ -110,6 +122,8 @@
     sub, lane = iota((8, LANES), 0), iota((8, LANES), 1)
     wide_sub, wide_lane = iota((LANES, LANES), 0), iota((LANES, LANES), 1)
     ranks = []
+    loads[0].wait()
+    loads[1].wait()
     for k in range(zones):
         owner = owner_ref[k : k + 1, :].astype(jnp.float32)
         patch = patch_ref[k : k + 1, :].astype(jnp.float32)
@@ -142,10 +156,10 @@
     lax.fori_loop(1, count, ask, 0)
     pltpu.make_async_copy(req_out.at[me], req_in.at[me], req_recv.at[zone]).start()
 
-    loads[0].wait()
+    loads[2].wait()
     packed[0:4, :] = table[8:12, 0 : half * LANES]
     packed[4:8, :] = table[8:12, half * LANES : tiles * LANES]
-    for load in loads[1:]:
+    for load in loads[3:]:
         load.wait()
 
     def stage(k, carry):
@@ -219,7 +233,7 @@
         lax.fori_loop(1 if dz == 0 else 0, peers, answer, 0)
 
     for k in range(zones):
-        live = lane[0:1] < count_ref[0, k]
+        live = lane[0:1] < count_ref[0:1, k : k + 1]
         cols = slice(k * LANES, (k + 1) * LANES)
 
         def keep(ref, row, value):
@@ -293,7 +307,7 @@
         accs = lax.fori_loop(0, LANES // 8, add, (zero,) * 16, unroll=2)
         sums = [jnp.sum(acc, axis=0, keepdims=True) for acc in accs]
         cols = slice(k * LANES, (k + 1) * LANES)
-        live = lane[0:1] < count_ref[0, k]
+        live = lane[0:1] < count_ref[0:1, k : k + 1]
         wgap = jnp.concatenate(sums[0:4], axis=0)
         active = active_ref[:, cols] == 1
         normal = nmult_ref[:, cols]
@@ -314,6 +328,18 @@
     pltpu.make_async_copy(sent, sent, req_send).wait()
     sent = rep_out.at[pl.ds(0, count - 1)]
     pltpu.make_async_copy(sent, sent, rep_send).wait()
+
+
+def deliver(*refs):
+    sources, targets, sem = refs[:5], refs[5:10], refs[10]
+    copies = [
+        pltpu.make_async_copy(source, target, sem.at[at])
+        for at, (source, target) in enumerate(zip(sources, targets))
+    ]
+    for copy in copies:
+        copy.start()
+    for copy in copies:
+        copy.wait()
 
 
 def local(
@@ -335,14 +361,13 @@
     patches = master_patch.shape[1]
     count = zones * peers
     f32 = jnp.float32
-    anywhere = pl.BlockSpec(memory_space=pl.ANY)
+    hbm = pl.BlockSpec(memory_space=pltpu.HBM)
     vmem = pl.BlockSpec(memory_space=pltpu.VMEM)
-    smem = pl.BlockSpec(memory_space=pltpu.SMEM)
     out = [jax.ShapeDtypeStruct((rows, slots), f32) for rows in (16, 16, 48, 4, 12)]
-    return pl.pallas_call(
+    results = pl.pallas_call(
         functools.partial(kernel, zones, peers),
         out_shape=out,
-        in_specs=[anywhere] * 5 + [vmem, vmem, smem, vmem, vmem, vmem],
+        in_specs=[hbm] * 11,
         out_specs=[vmem] * 5,
         scratch_shapes=[
             pltpu.VMEM((slots, gauss), f32),
@@ -351,19 +376,25 @@
             pltpu.VMEM((3, slots, gauss), f32),
             pltpu.VMEM((12, patches), f32),
             pltpu.VMEM((8, patches // 2), f32),
+            pltpu.VMEM((zones, block), jnp.int32),
+            pltpu.VMEM((zones, block), jnp.int32),
+            pltpu.VMEM((1, zones), jnp.int32),
+            pltpu.VMEM((4, slots), jnp.int32),
+            pltpu.VMEM((4, slots), f32),
+            pltpu.VMEM((12, slots), f32),
             pltpu.VMEM((18, zones, gauss, block), f32),
             pltpu.VMEM((count, 1, LANES), jnp.int32),
             pltpu.VMEM((count, 1, LANES), jnp.int32),
             pltpu.VMEM((count, 1, 2 * LANES), f32),
             pltpu.VMEM((count, 1, 2 * LANES), f32),
-            pltpu.SemaphoreType.DMA((5,)),
+            pltpu.SemaphoreType.DMA((11,)),
             pltpu.SemaphoreType.DMA,
             pltpu.SemaphoreType.DMA((zones,)),
             pltpu.SemaphoreType.DMA,
             pltpu.SemaphoreType.DMA((zones,)),
         ],
         compiler_params=pltpu.CompilerParams(
-            collective_id=0, has_side_effects=True, vmem_limit_bytes=40 * 2**20
+            collective_id=0, has_side_effects=True
         ),
     )(
         quad_weight,
@@ -378,6 +409,13 @@
         normal_mult,
         tangent_mult,
     )
+    return pl.pallas_call(
+        deliver,
+        out_shape=out,
+        in_specs=[vmem] * 5,
+        out_specs=[hbm] * 5,
+        scratch_shapes=[pltpu.SemaphoreType.DMA((5,))],
+    )(*results)
 
 
 def solution(mesh):

time: 32 us -> 21.3 us (0.67); the launches traced: 31.5 us -> 21.2 us
  local copies, waits for them, and re-layouts: 12.1 us -> 0 us
  Pallas kernels: 18.8 us -> 20.5 us
    unnamed x27 -> x0, local copies, waits for them, and re-layouts: 12.1 us -> none
    pallas_call x0 -> x1, Pallas kernels: none -> 1.67 us  [local(): pl.pallas_call(deliver, out_shape=out, in_specs=[vmem] * 5, out_specs=[hb...]
where the time goes in v3:
time: 21.3 us; the launch traced here: 21.2 us
  Pallas kernels  20.5 us (96%)
  between operations  0.64 us (3%)
    pallas_call x1, Pallas kernels, local(): pl.pallas_call(functools.partial(kernel, zones, peers), out_shape=out, in...  18.9 us
    pallas_call x1, Pallas kernels, local(): pl.pallas_call(deliver, out_shape=out, in_specs=[vmem] * 5, out_specs=[hb...  1.67 us

profile of v3, /device:TPU:0, one launch (start us, length us, event | category | flops | bytes accessed | tf_op | source)
XLA Modules:
  0.0 21.2 jit_solution(17323744628771230323)
XLA Ops:
  0.6 18.9 %shard_map.146 = (f32[16,512]{1,0:T(8,128)}, f32[16,512]{1,0:T(8,128)}, f32[48,512]{1,0:T(8,128)}, f32[4,512]{1,0:T(4,128)}, f32[12,512]{1,0:T(8,128)}) custom-call(f32[512,128]{1,0:T(8,128)} %quad_hbm.1, f32[2048,128]{1,0:T(8,128)} %bitcast.5, f32[3,512,128]{2,1,0:T(8,128)} %bitcast.6, f32[3,512,128]{2,1,0:T(8,128)} %bitcast.7, f32[12,8192]{1,0:T(8,128)} %master_hbm.1, ...), custom_call_target="tpu_custom_call" | custom-call | tf_op jit(solution)/shard_map/pallas_call | solution.py:367
  19.5 1.7 %shard_map.147 = (f32[16,512]{1,0:T(8,128)}, f32[16,512]{1,0:T(8,128)}, f32[48,512]{1,0:T(8,128)}, f32[4,512]{1,0:T(4,128)}, f32[12,512]{1,0:T(8,128)}) custom-call(f32[16,512]{1,0:T(8,128)} %get-tuple-element.10.refs_0_, f32[16,512]{1,0:T(8,128)} %get-tuple-element.11.refs_1_, f32[48,512]{1,0:T(8,128)} %get-tuple-element.12.refs_2_, ...), custom_call_target="tpu_custom_call" | custom-call | tf_op jit(solution)/shard_map/pallas_call | solution.py:412

commit v4 on v3

--- a/solution.py
+++ b/solution.py
@@ -66,6 +66,7 @@
     active_ref,
     nmult_ref,
     tmult_ref,
+    rank_ref,
     terms,
     req_out,
     req_in,
@@ -83,6 +84,20 @@
     me = zone * peers + dev
     tiles = table.shape[1] // LANES
     half = tiles // 2
+
+    barrier = pltpu.get_barrier_semaphore()
+
+    def greet(step, carry):
+        other = lax.rem(me + step, count)
+        pl.semaphore_signal(
+            barrier,
+            inc=1,
+            device_id=(lax.div(other, peers), lax.rem(other, peers)),
+            device_id_type=MESH,
+        )
+        return carry
+
+    lax.fori_loop(1, count, greet, 0)
 
     loads = [
         pltpu.make_async_copy(source, target, load_sem.at[at])
@@ -105,23 +120,8 @@
     for load in loads:
         load.start()
 
-    barrier = pltpu.get_barrier_semaphore()
-
-    def greet(step, carry):
-        other = lax.rem(me + step, count)
-        pl.semaphore_signal(
-            barrier,
-            inc=1,
-            device_id=(lax.div(other, peers), lax.rem(other, peers)),
-            device_id_type=MESH,
-        )
-        return carry
-
-    lax.fori_loop(1, count, greet, 0)
-
     sub, lane = iota((8, LANES), 0), iota((8, LANES), 1)
     wide_sub, wide_lane = iota((LANES, LANES), 0), iota((LANES, LANES), 1)
-    ranks = []
     loads[0].wait()
     loads[1].wait()
     for k in range(zones):
@@ -130,7 +130,7 @@
         across = jnp.broadcast_to(owner, (LANES, LANES))
         same = (across.T == across) & (wide_sub < wide_lane)
         rank = jnp.sum(jnp.where(same, 1.0, 0.0), axis=0, keepdims=True).astype(jnp.int32)
-        ranks.append(rank)
+        rank_ref[k : k + 1, :] = rank
         place = owner_ref[k : k + 1, :] * BUCKET + rank
         for g in range(groups):
             chosen = jnp.where(wide_sub + g * LANES == place, jnp.broadcast_to(patch, (LANES, LANES)), 0.0)
@@ -141,20 +141,24 @@
 
     pl.semaphore_wait(barrier, count - 1)
 
-    def ask(step, carry):
-        other = lax.rem(me + step, count)
-        pltpu.make_async_remote_copy(
-            src_ref=req_out.at[other],
-            dst_ref=req_in.at[me],
-            send_sem=req_send,
-            recv_sem=req_recv.at[zone],
-            device_id=(lax.div(other, peers), lax.rem(other, peers)),
-            device_id_type=MESH,
-        ).start()
-        return carry
-
-    lax.fori_loop(1, count, ask, 0)
-    pltpu.make_async_copy(req_out.at[me], req_in.at[me], req_recv.at[zone]).start()
+    for dz in range(zones):
+        target = lax.rem(zone - dz + zones, zones)
+
+        def ask(step, carry):
+            peer = lax.rem(dev + step, peers)
+            pltpu.make_async_remote_copy(
+                src_ref=req_out.at[target * peers + peer],
+                dst_ref=req_in.at[me],
+                send_sem=req_send,
+                recv_sem=req_recv.at[zone],
+                device_id=(target, peer),
+                device_id_type=MESH,
+            ).start()
+            return carry
+
+        if dz == 0:
+            pltpu.make_async_copy(req_out.at[me], req_in.at[me], req_recv.at[zone]).start()
+        lax.fori_loop(1 if dz == 0 else 0, peers, ask, 0)
 
     loads[2].wait()
     packed[0:4, :] = table[8:12, 0 : half * LANES]
@@ -264,11 +268,11 @@
     undo = ((((lane >> 4) - sub) & 7) << 4) + (lane & 15)
     mix = ((lane >> 4) - sub - turn) & 7
     for dz in range(zones):
-        k = dz
+        k = lax.rem(zone - dz + zones, zones)
         whole = rep_in.at[pl.ds(k * peers, peers)]
         pltpu.make_async_copy(whole, whole, rep_recv.at[k]).wait()
-        owner = jnp.broadcast_to(owner_ref[k : k + 1, :], (8, LANES))
-        seat = (((owner + sub + turn) & 7) << 4) + jnp.broadcast_to(ranks[k], (8, LANES))
+        owner = jnp.broadcast_to(owner_ref[pl.ds(k, 1), :], (8, LANES))
+        seat = (((owner + sub + turn) & 7) << 4) + jnp.broadcast_to(rank_ref[pl.ds(k, 1), :], (8, LANES))
         found = []
         for h in range(2):
             total = jnp.zeros((8, LANES), jnp.float32)
@@ -306,8 +310,9 @@
         zero = jnp.zeros((8, LANES), jnp.float32)
         accs = lax.fori_loop(0, LANES // 8, add, (zero,) * 16, unroll=2)
         sums = [jnp.sum(acc, axis=0, keepdims=True) for acc in accs]
-        cols = slice(k * LANES, (k + 1) * LANES)
-        live = lane[0:1] < count_ref[0:1, k : k + 1]
+        cols = pl.ds(pl.multiple_of(k * LANES, LANES), LANES)
+        group = jnp.where(iota((1, zones), 1) == k, count_ref[...], 0)
+        live = lane[0:1] < jnp.sum(group, axis=1, keepdims=True)
         wgap = jnp.concatenate(sums[0:4], axis=0)
         active = active_ref[:, cols] == 1
         normal = nmult_ref[:, cols]
@@ -382,6 +387,7 @@
             pltpu.VMEM((4, slots), jnp.int32),
             pltpu.VMEM((4, slots), f32),
             pltpu.VMEM((12, slots), f32),
+            pltpu.VMEM((zones, block), jnp.int32),
             pltpu.VMEM((18, zones, gauss, block), f32),
             pltpu.VMEM((count, 1, LANES), jnp.int32),
             pltpu.VMEM((count, 1, LANES), jnp.int32),
@@ -394,9 +400,9 @@
             pltpu.SemaphoreType.DMA((zones,)),
         ],
         compiler_params=pltpu.CompilerParams(
-            collective_id=0, has_side_effects=True
+            collective_id=0, has_side_effects=True, vmem_limit_bytes=36 * 2**20
         ),
-    )(
+    )(*[pltpu.with_memory_space_constraint(x, pltpu.HBM) for x in (
         quad_weight,
         param_coords.reshape(4 * slots, gauss),
         slave_points.transpose(1, 0, 2),
@@ -408,13 +414,14 @@
         active_flags,
         normal_mult,
         tangent_mult,
-    )
+    )])
     return pl.pallas_call(
         deliver,
         out_shape=out,
         in_specs=[vmem] * 5,
         out_specs=[hbm] * 5,
         scratch_shapes=[pltpu.SemaphoreType.DMA((5,))],
+        compiler_params=pltpu.CompilerParams(vmem_limit_bytes=8 * 2**20),
     )(*results)
 
 

time: 21.3 us -> 19.2 us (0.901)
  Pallas kernels: 20.5 us -> 18.4 us
    pallas_call x1, Pallas kernels: 18.9 us -> 17.7 us  [local(): pl.pallas_call(functools.partial(kernel, zones, peers), out_shape=out, in...]
    pallas_call x1, Pallas kernels: 1.67 us -> 0.72 us  [local(): pl.pallas_call(deliver, out_shape=out, in_specs=[vmem] * 5, out_specs=[hb...]
where the time goes in v4:
time: 19.2 us; the launch traced here: 19.1 us
  Pallas kernels  18.4 us (96%)
  between operations  0.64 us (3%)
    pallas_call x1, Pallas kernels, local(): pl.pallas_call(functools.partial(kernel, zones, peers), out_shape=out, in...  17.7 us
    pallas_call x1, Pallas kernels, local(): pl.pallas_call(deliver, out_shape=out, in_specs=[vmem] * 5, out_specs=[hb...  0.72 us

profile of v4, /device:TPU:0, one launch (start us, length us, event | category | flops | bytes accessed | tf_op | source)
XLA Modules:
  0.0 19.1 jit_solution(13906872495147889461)
XLA Ops:
  0.6 17.7 %shard_map.146 = (f32[16,512]{1,0:T(8,128)S(1)}, f32[16,512]{1,0:T(8,128)S(1)}, f32[48,512]{1,0:T(8,128)S(1)}, f32[4,512]{1,0:T(4,128)S(1)}, f32[12,512]{1,0:T(8,128)S(1)}) custom-call(f32[512,128]{1,0:T(8,128)} %quad_hbm.1, f32[2048,128]{1,0:T(8,128)} %bitcast.5, f32[3,512,128]{2,1,0:T(8,128)} %bitcast.6, f32[3,512,128]{2,1,0:T(8,128)} %bitcast.7, ...), custom_call_target="tpu_custom_call" | custom-call | tf_op jit(solution)/shard_map/pallas_call | solution.py:372
  18.3 0.7 %shard_map.147 = (f32[16,512]{1,0:T(8,128)}, f32[16,512]{1,0:T(8,128)}, f32[48,512]{1,0:T(8,128)}, f32[4,512]{1,0:T(4,128)}, f32[12,512]{1,0:T(8,128)}) custom-call(f32[16,512]{1,0:T(8,128)S(1)} %get-tuple-element.10.refs_0_, f32[16,512]{1,0:T(8,128)S(1)} %get-tuple-element.11.refs_1_, f32[48,512]{1,0:T(8,128)S(1)} %get-tuple-element.12.refs_2_, ...), custom_call_target="tpu_custom_call" | custom-call | tf_op jit(solution)/shard_map/pallas_call | solution.py:418
